TPU v7x, 32 devices: a whole 2x2x4 slice. The times are simulated.
32 devices in a mesh: pair: 8 (over y, x, core), grp: 4 (over z).
Axes of the slice: x: 2, y: 2, z: 4, core: 2. Of those that a mesh axis runs over, the one named last changes fastest.
Arguments:
- sector_rows: int32 [4], replicated, may hold values from 1 to 256, 768 in all
- wavefunction: bfloat16 [4, 256, 512], P('grp'), may hold values from -6 to 6
- left_ops: bfloat16 [64, 4, 256, 256], P(('pair', 'grp')), may hold values from -0.375 to 0.375
- right_diag: bfloat16 [64, 4, 512], P('pair', 'grp'), may hold values from -0.0078125 to 0.0078125
Outputs:
- slab: float32 [64, 64], P(('pair', 'grp'))
Inputs may be any that keep to these rules, and one draw needn't show every extreme that they name: `sector_rows`: each entry counts the live leading rows of one sector block; at least one sector has 256.
All inputs are finite; a program needn't handle non-finite values.
Results may differ from a plain program's by a relative error of at most 0.0029.
Values may be sent and summed in bfloat16 or wider, within the bound.
No kernel may reach another device: no remote copies, remote signals or barrier semaphores. Data moves between devices by JAX's collectives and lax.ppermute only.
A program may use at most 64 MiB of HBM per device.

v0:
```python
import jax
import jax.numpy as jnp
from jax import lax
from jax.sharding import PartitionSpec as P


def live_states(sector_rows, wavefunction):
    row_index = lax.broadcasted_iota(jnp.int32, wavefunction.shape, 1)
    return jnp.where(
        row_index < sector_rows[:, None, None], wavefunction, jnp.zeros_like(wavefunction)
    )


def local(sector_rows, wavefunction, left_ops, right_diag):
    owned = wavefunction.shape[0]
    first = lax.axis_index("grp") * owned
    right_local = lax.all_gather(right_diag, "pair", axis=0, tiled=True)
    own_rows = lax.dynamic_slice_in_dim(sector_rows, first, owned, 0)
    live = live_states(own_rows, wavefunction)
    blocks = lax.all_to_all(left_ops, "grp", split_axis=1, concat_axis=0, tiled=True)

    def per_pair(block):
        image = jnp.einsum("sab,sbc->sac", block, live, preferred_element_type=jnp.float32)
        return jnp.sum(live.astype(jnp.float32) * image, axis=1)

    weights = lax.map(per_pair, blocks).astype(jnp.bfloat16)
    group_pairs = weights.shape[0]
    flat = weights.reshape(group_pairs, -1)
    diag_flat = right_local.reshape(right_local.shape[0], -1)
    partial_slab = lax.dot_general(
        flat, diag_flat, (((1,), (1,)), ((), ())), preferred_element_type=jnp.float32
    )
    result = lax.psum_scatter(partial_slab, "grp", scatter_dimension=0, tiled=True)
    return result


def solution(mesh):
    in_specs = (
        P(),
        P("grp", None, None),
        P(("pair", "grp"), None, None, None),
        P("pair", "grp", None),
    )
    out_specs = P(("pair", "grp"), None)
    return jax.shard_map(local, mesh=mesh, in_specs=in_specs, out_specs=out_specs, check_vma=False)
```

profile of v0, /device:TPU:0, one launch (start us, length us, event | category | flops | bytes accessed | tf_op | source)
XLA Modules:
  0.0 47.5 jit_solution(5526043052721479483)
XLA Ops:
  0.0 2.3 %copy.8 = bf16[2,4,256,256]{3,2,0,1:T(8,128)(2,1)} copy(bf16[2,4,256,256]{3,2,1,0:T(8,128)(2,1)} %param.8) | data formatting | bytes 2097152 | tf_op args[2]
  2.3 0.0 copy-start.3
  2.3 0.0 copy-start
  2.3 6.5 %all-to-all-start = ((bf16[2,4,256,256]{3,2,0,1:T(8,128)(2,1)}), bf16[2,4,256,256]{3,2,0,1:T(8,128)(2,1)S(1)}, u32[]{:S(2)}, u32[]{:S(2)}) async-start(bf16[2,4,256,256]{3,2,0,1:T(8,128)(2,1)} %copy.8), calls=%async_computation | async-start | bytes 2097152 | tf_op jit(solution)/shard_map/all_to_all | solution.py:20
  8.8 0.0 copy-start.2
  8.8 0.7 %copy-done.2 = s32[4]{0:T(128)S(1)} copy-done((s32[4]{0:T(128)S(1)}, s32[4]{0:T(128)}, u32[]{:S(2)}) %copy-start.2) | copy-done | bytes 40
  9.4 0.6 %dynamic_slice.7 = s32[1]{0:T(128)} dynamic-slice(s32[4]{0:T(128)S(1)} %copy-done.2, s32[]{:T(128)S(6)} %select_n.7), dynamic_slice_sizes={1} | dynamic-slice | bytes 12 | tf_op jit(solution)/shard_map/dynamic_slice | solution.py:18
  10.0 0.0 copy-start.1
  10.0 0.0 copy-done.3
  10.0 0.6 %dynamic-slice = u32[1]{0:T(128)} dynamic-slice(u32[32]{0:T(128)S(1)} %copy-done.3, u32[]{:T(128)S(6)} %add.10), dynamic_slice_sizes={1} | dynamic-slice | bytes 12
  11.3 0.0 copy-done.1
  11.3 9.3 %all_gather.3 = bf16[64,1,512]{2,0,1:T(8,128)(2,1)S(1)} all-gather(bf16[8,1,512]{2,0,1:T(8,128)(2,1)S(1)} %copy-done.1), channel_id=1, replica_groups=mesh['pair'=8,'grp'=4] {'pair'}, dimensions={0}, use_global_device_ids=true | all-gather | bytes 73728 | tf_op jit(solution)/shard_map/all_gather | solution.py:17
  20.6 0.0 copy-done
  20.6 0.7 %fusion.5 = bf16[1,256,512]{2,1,0:T(8,128)(2,1)S(1)} fusion(bf16[1,256,512]{2,1,0:T(8,128)(2,1)S(1)} %copy-done, s32[]{:T(128)} %bitcast.3), kind=kLoop, calls=%fused_computation.7 | loop fusion | flops 262144 | bytes 524292 | tf_op jit(solution)/shard_map/jit(_where)/select_n | solution.py:9
  21.3 13.2 %all-to-all-done = bf16[2,4,256,256]{3,2,0,1:T(8,128)(2,1)S(1)} async-done(((bf16[2,4,256,256]{3,2,0,1:T(8,128)(2,1)}), bf16[2,4,256,256]{3,2,0,1:T(8,128)(2,1)S(1)}, u32[]{:S(2)}, u32[]{:S(2)}) %all-to-all-start) | async-done | bytes 1048608 | tf_op jit(solution)/shard_map/all_to_all | solution.py:20
  34.5 2.5 %while.10 = (s32[]{:T(128)}, bf16[8,1,512]{2,0,1:T(8,128)(2,1)S(1)}, bf16[1,256,512]{2,1,0:T(8,128)(2,1)S(1)}, bf16[8,1,256,256]{3,2,1,0:T(8,128)(2,1)S(1)}, s32[]{:T(128)}, /*index=5*/s32[]{:T(128)}) while((s32[]{:T(128)}, bf16[8,1,512]{2,0,1:T(8,128)(2,1)S(1)}, bf16[1,256,512]{2,1,0:T(8,128)(2,1)S(1)}, ...), condition=%wide.region_2.3_spmd, body=%wide.region_0.2_spmd.sunk | while | flops 67501568 | bytes 661581 | solution.py:26
  34.5 0.2 fusion.15
  34.8 0.2 fusion.15
  35.1 0.2 fusion.15
  35.4 0.2 fusion.15
  35.7 0.2 fusion.15
  36.0 0.2 fusion.15
  36.3 0.2 fusion.15
  36.7 0.2 fusion.15
  37.0 0.1 fusion.6
  37.1 9.8 %all-reduce = f32[8,64]{1,0:T(8,128)S(1)} all-reduce(f32[8,64]{1,0:T(8,128)S(1)} %fusion.6), channel_id=2, replica_groups=mesh['pair'=8,'grp'=4] {'grp'}, use_global_device_ids=true, to_apply=%region_3.4.clone | all-reduce | flops 512 | bytes 4096
  46.9 0.6 %constant_dynamic-slice_fusion = f32[2,64]{1,0:T(2,128)} fusion(f32[8,64]{1,0:T(8,128)S(1)} %all-reduce, u32[]{:T(128)S(6)} %multiply.1), kind=kLoop, calls=%fused_computation.12 | loop fusion | bytes 1028
  (9 shorter events, 0.3 us)
Async XLA Ops:
  2.3 7.8 %copy-start.3 = (u32[32]{0:T(128)S(1)}, u32[32]{0:T(128)}, u32[]{:S(2)}) copy-start(u32[32]{0:T(128)} %constant.28) | copy-start | bytes 388
  2.3 18.3 %copy-start = (bf16[1,256,512]{2,1,0:T(8,128)(2,1)S(1)}, bf16[1,256,512]{2,1,0:T(8,128)(2,1)}, u32[]{:S(2)}) copy-start(bf16[1,256,512]{2,1,0:T(8,128)(2,1)} %param.7) | copy-start | bytes 786436
  2.3 32.2 %all-to-all-start = ((bf16[2,4,256,256]{3,2,0,1:T(8,128)(2,1)}), bf16[2,4,256,256]{3,2,0,1:T(8,128)(2,1)S(1)}, u32[]{:S(2)}, u32[]{:S(2)}) async-start(bf16[2,4,256,256]{3,2,0,1:T(8,128)(2,1)} %copy.8), calls=%async_computation | async-start | bytes 2097152 | tf_op jit(solution)/shard_map/all_to_all | solution.py:20
  8.8 0.7 %copy-start.2 = (s32[4]{0:T(128)S(1)}, s32[4]{0:T(128)}, u32[]{:S(2)}) copy-start(s32[4]{0:T(128)} %param.6) | copy-start | bytes 52
  10.0 1.3 %copy-start.1 = (bf16[8,1,512]{2,0,1:T(8,128)(2,1)S(1)}, bf16[8,1,512]{2,0,1:T(8,128)(2,1)}, u32[]{:S(2)}) copy-start(bf16[8,1,512]{2,0,1:T(8,128)(2,1)} %param.9) | copy-start | bytes 24580
where the time goes:
time: 47.7 us; the launch traced here: 47.5 us
  blocking collectives  19.1 us (40%)
  waiting for transfers between devices  13.2 us (28%)
  starting transfers between devices  6.48 us (14%)
  local copies, waits for them, and re-layouts  5.1 us (11%)
  matrix products  2.07 us (4%)
  other arithmetic  0.7 us (1%)
  between operations  0.67 us (1%)
    all_to_all x1, waiting for transfers between devices, local(): lax.all_to_all(left_ops, 'grp', split_axis=1, concat_axis=0, tiled=True)  13.2 us
    unnamed x1, blocking collectives  9.81 us
    all_gather x1, blocking collectives, local(): right_local = lax.all_gather(right_diag, 'pair', axis=0, tiled=True)  9.26 us
    all_to_all x1, starting transfers between devices, local(): lax.all_to_all(left_ops, 'grp', split_axis=1, concat_axis=0, tiled=True)  6.48 us
    unnamed x11, local copies, waits for them, and re-layouts  4.15 us
    dot_general x8, matrix products, per_pair(): jnp.einsum('sab,sbc->sac', block, live, preferred_element_type=jnp.float32)  1.95 us
  transfers between devices with their start and end apart: 1, of which 1 were waited for; matrix products, arithmetic and copies ran while one was open for 4% of the time, Pallas kernels for 0%

commit v1 on v0

--- a/solution.py
+++ b/solution.py
@@ -17,7 +17,19 @@
     right_local = lax.all_gather(right_diag, "pair", axis=0, tiled=True)
     own_rows = lax.dynamic_slice_in_dim(sector_rows, first, owned, 0)
     live = live_states(own_rows, wavefunction)
-    blocks = lax.all_to_all(left_ops, "grp", split_axis=1, concat_axis=0, tiled=True)
+    ways, here = (lax.axis_size("grp"), lax.axis_index("grp"))
+    width = left_ops.shape[1] // ways
+    shape = list(left_ops.shape)
+    shape[1] = width
+    height = shape[0]
+    shape[0] = height * ways
+    full = jnp.zeros(shape, left_ops.dtype)
+    for mask in range(ways):
+        part = lax.dynamic_slice_in_dim(left_ops, (here ^ mask) * width, width, axis=1)
+        if mask:
+            part = lax.ppermute(part, "grp", [(d, d ^ mask) for d in range(ways)])
+        full = lax.dynamic_update_slice_in_dim(full, part, (here ^ mask) * height, axis=0)
+    blocks = full
 
     def per_pair(block):
         image = jnp.einsum("sab,sbc->sac", block, live, preferred_element_type=jnp.float32)

time: 47.7 us -> 42.3 us (0.89)
  waiting for transfers between devices: 13.2 us -> 6.02 us
  blocking collectives: 19.1 us -> 22.6 us
  local copies, waits for them, and re-layouts: 5.1 us -> 4.05 us
  starting transfers between devices: 6.48 us -> 5.71 us
    all_to_all x1 -> x0, waiting for transfers between devices: 13.2 us -> none  [local(): lax.all_to_all(left_ops, 'grp', split_axis=1, concat_axis=0, tiled=True)]
    all_to_all x1 -> x0, starting transfers between devices: 6.48 us -> none  [local(): lax.all_to_all(left_ops, 'grp', split_axis=1, concat_axis=0, tiled=True)]
    ppermute x0 -> x3, waiting for transfers between devices: none -> 6.02 us  [local(): part = lax.ppermute(part, 'grp', [(d, d ^ mask) for d in range(ways)])]
    ppermute x0 -> x3, starting transfers between devices: none -> 5.71 us  [local(): part = lax.ppermute(part, 'grp', [(d, d ^ mask) for d in range(ways)])]
    unnamed x1, blocking collectives: 9.81 us -> 13.1 us
    unnamed x11 -> x12, local copies, waits for them, and re-layouts: 4.15 us -> 2.92 us
  transfers between devices with their start and end apart: 1 -> 3, of which waited for: 1 -> 1; matrix products, arithmetic and copies ran while one was open for 4% -> 5% of each run, Pallas kernels for 0% -> 0%
where the time goes in v1:
time: 42.3 us; the launch traced here: 42.1 us
  blocking collectives  22.6 us (53%)
  waiting for transfers between devices  6.02 us (14%)
  starting transfers between devices  5.71 us (13%)
  local copies, waits for them, and re-layouts  4.05 us (10%)
  matrix products  2.08 us (5%)
  between operations  0.75 us (2%)
  other arithmetic  0.71 us (2%)
    unnamed x1, blocking collectives  13.1 us
    all_gather x1, blocking collectives, local(): right_local = lax.all_gather(right_diag, 'pair', axis=0, tiled=True)  9.48 us
    ppermute x3, waiting for transfers between devices, local(): part = lax.ppermute(part, 'grp', [(d, d ^ mask) for d in range(ways)])  6.02 us
    ppermute x3, starting transfers between devices, local(): part = lax.ppermute(part, 'grp', [(d, d ^ mask) for d in range(ways)])  5.71 us
    unnamed x12, local copies, waits for them, and re-layouts  2.92 us
    dot_general x8, matrix products, per_pair(): jnp.einsum('sab,sbc->sac', block, live, preferred_element_type=jnp.float32)  1.95 us
  transfers between devices with their start and end apart: 3, of which 1 were waited for; matrix products, arithmetic and copies ran while one was open for 5% of the time, Pallas kernels for 0%

profile of v1, /device:TPU:0, one launch (start us, length us, event | category | flops | bytes accessed | tf_op | source)
XLA Modules:
  0.0 42.1 jit_solution(16885321399417180998)
XLA Ops:
  0.0 0.0 copy-start
  0.0 0.1 broadcast_in_dim.16
  0.1 1.1 %copy-done = bf16[2,4,256,256]{3,2,1,0:T(8,128)(2,1)S(1)} copy-done((bf16[2,4,256,256]{3,2,1,0:T(8,128)(2,1)S(1)}, bf16[2,4,256,256]{3,2,1,0:T(8,128)(2,1)}, u32[]{:S(2)}) %copy-start) | copy-done | bytes 1048600
  1.2 0.0 copy-start.1
  1.2 0.1 constant_dynamic-slice_fusion
  1.3 3.1 %collective-permute-start = (bf16[2,1,256,256]{3,2,1,0:T(8,128)(2,1)S(1)}, bf16[2,1,256,256]{3,2,1,0:T(8,128)(2,1)S(1)}, u32[]{:S(2)}, u32[]{:S(2)}) collective-permute-start(bf16[2,1,256,256]{3,2,1,0:T(8,128)(2,1)S(1)} %get-tuple-element.37), channel_id=1, source_target_pairs={{0,1},{1,0},{2,3},{3,2},{4,5},{5,4},{6,7},{7,6},{8,9},{9,8},{10,11... | collective-permute-start | bytes 786440 | tf_op jit(solution)/shard_map/ppermute | solution.py:30
  4.4 0.0 copy-start.3
  4.4 2.6 %collective-permute-start.1 = (bf16[2,1,256,256]{3,2,1,0:T(8,128)(2,1)S(1)}, bf16[2,1,256,256]{3,2,1,0:T(8,128)(2,1)S(1)}, u32[]{:S(2)}, u32[]{:S(2)}) collective-permute-start(bf16[2,1,256,256]{3,2,1,0:T(8,128)(2,1)S(1)} %get-tuple-element.39), channel_id=1, source_target_pairs={{0,2},{1,3},{2,0},{3,1},{4,6},{5,7},{6,4},{7,5},{8,10},{9,11},{10,... | collective-permute-start | bytes 786440 | tf_op jit(solution)/shard_map/ppermute | solution.py:30
  7.0 0.0 collective-permute-start.2
  7.0 0.0 copy-done.3
  7.0 0.6 %dynamic_slice.19 = s32[1]{0:T(128)} dynamic-slice(s32[4]{0:T(128)S(1)} %copy-done.3, s32[]{:T(128)S(6)} %select_n.29), dynamic_slice_sizes={1} | dynamic-slice | bytes 12 | tf_op jit(solution)/shard_map/dynamic_slice | solution.py:18
  7.6 0.0 copy-done.1
  7.6 0.7 %fusion.5 = bf16[1,256,512]{2,1,0:T(8,128)(2,1)S(1)} fusion(bf16[1,256,512]{2,1,0:T(8,128)(2,1)S(1)} %copy-done.1, s32[]{:T(128)} %bitcast.3), kind=kLoop, calls=%fused_computation.7 | loop fusion | flops 262144 | bytes 524292 | tf_op jit(solution)/shard_map/jit(_where)/select_n | solution.py:9
  8.3 0.0 copy-start.4
  8.4 0.0 copy-start.2
  8.4 0.6 %copy-done.4 = u32[32]{0:T(128)S(1)} copy-done((u32[32]{0:T(128)S(1)}, u32[32]{0:T(128)}, u32[]{:S(2)}) %copy-start.4) | copy-done | bytes 152
  9.0 0.6 %dynamic-slice = u32[1]{0:T(128)} dynamic-slice(u32[32]{0:T(128)S(1)} %copy-done.4, u32[]{:T(128)S(6)} %add.39), dynamic_slice_sizes={1} | dynamic-slice | bytes 12
  10.2 0.0 copy-done.2
  10.2 9.5 %all_gather.3 = bf16[64,1,512]{2,0,1:T(8,128)(2,1)S(1)} all-gather(bf16[8,1,512]{2,0,1:T(8,128)(2,1)S(1)} %copy-done.2), channel_id=1, replica_groups=mesh['pair'=8,'grp'=4] {'pair'}, dimensions={0}, use_global_device_ids=true | all-gather | bytes 73728 | tf_op jit(solution)/shard_map/all_gather | solution.py:17
  19.7 0.0 collective-permute-done
  19.7 6.0 %collective-permute-done.1 = bf16[2,1,256,256]{3,2,1,0:T(8,128)(2,1)S(1)} collective-permute-done((bf16[2,1,256,256]{3,2,1,0:T(8,128)(2,1)S(1)}, bf16[2,1,256,256]{3,2,1,0:T(8,128)(2,1)S(1)}, u32[]{:S(2)}, u32[]{:S(2)}) %collective-permute-start.1) | collective-permute-done | bytes 262176 | tf_op jit(solution)/shard_map/ppermute | solution.py:30
  25.8 0.0 collective-permute-done.2
  25.8 2.5 %while.10 = (s32[]{:T(128)}, bf16[8,1,512]{2,0,1:T(8,128)(2,1)S(1)}, bf16[1,256,512]{2,1,0:T(8,128)(2,1)S(1)}, bf16[8,1,256,256]{3,2,1,0:T(8,128)(2,1)S(1)}, s32[]{:T(128)}, /*index=5*/s32[]{:T(128)}) while((s32[]{:T(128)}, bf16[8,1,512]{2,0,1:T(8,128)(2,1)S(1)}, bf16[1,256,512]{2,1,0:T(8,128)(2,1)S(1)}, ...), condition=%wide.region_2.3_spmd, body=%wide.region_0.2_spmd.sunk | while | flops 67501568 | bytes 661581 | solution.py:38
  25.8 0.2 fusion.15
  26.1 0.2 fusion.15
  26.4 0.2 fusion.15
  26.7 0.2 fusion.15
  27.1 0.2 fusion.15
  27.4 0.2 fusion.15
  27.7 0.2 fusion.15
  28.0 0.2 fusion.15
  28.3 0.1 fusion.6
  28.4 13.1 %all-reduce = f32[8,64]{1,0:T(8,128)S(1)} all-reduce(f32[8,64]{1,0:T(8,128)S(1)} %fusion.6), channel_id=2, replica_groups=mesh['pair'=8,'grp'=4] {'grp'}, use_global_device_ids=true, to_apply=%region_3.4.clone | all-reduce | flops 512 | bytes 4096
  41.5 0.6 %constant_dynamic-slice_fusion.3 = f32[2,64]{1,0:T(2,128)} fusion(f32[8,64]{1,0:T(8,128)S(1)} %all-reduce, u32[]{:T(128)S(6)} %multiply.1), kind=kLoop, calls=%fused_computation.19 | loop fusion | bytes 1028
  (12 shorter events, 0.4 us)
Async XLA Ops:
  0.0 1.2 %copy-start = (bf16[2,4,256,256]{3,2,1,0:T(8,128)(2,1)S(1)}, bf16[2,4,256,256]{3,2,1,0:T(8,128)(2,1)}, u32[]{:S(2)}) copy-start(bf16[2,4,256,256]{3,2,1,0:T(8,128)(2,1)} %param.8) | copy-start | bytes 3145732
  1.2 6.4 %copy-start.1 = (bf16[1,256,512]{2,1,0:T(8,128)(2,1)S(1)}, bf16[1,256,512]{2,1,0:T(8,128)(2,1)}, u32[]{:S(2)}) copy-start(bf16[1,256,512]{2,1,0:T(8,128)(2,1)} %param.7) | copy-start | bytes 786436
  1.3 18.4 %collective-permute-start = (bf16[2,1,256,256]{3,2,1,0:T(8,128)(2,1)S(1)}, bf16[2,1,256,256]{3,2,1,0:T(8,128)(2,1)S(1)}, u32[]{:S(2)}, u32[]{:S(2)}) collective-permute-start(bf16[2,1,256,256]{3,2,1,0:T(8,128)(2,1)S(1)} %get-tuple-element.37), channel_id=1, source_target_pairs={{0,1},{1,0},{2,3},{3,2},{4,5},{5,4},{6,7},{7,6},{8,9},{9,8},{10,11... | collective-permute-start | bytes 786440 | tf_op jit(solution)/shard_map/ppermute | solution.py:30
  4.4 2.6 %copy-start.3 = (s32[4]{0:T(128)S(1)}, s32[4]{0:T(128)}, u32[]{:S(2)}) copy-start(s32[4]{0:T(128)} %param.6) | copy-start | bytes 52
  4.4 21.3 %collective-permute-start.1 = (bf16[2,1,256,256]{3,2,1,0:T(8,128)(2,1)S(1)}, bf16[2,1,256,256]{3,2,1,0:T(8,128)(2,1)S(1)}, u32[]{:S(2)}, u32[]{:S(2)}) collective-permute-start(bf16[2,1,256,256]{3,2,1,0:T(8,128)(2,1)S(1)} %get-tuple-element.39), channel_id=1, source_target_pairs={{0,2},{1,3},{2,0},{3,1},{4,6},{5,7},{6,4},{7,5},{8,10},{9,11},{10,... | collective-permute-start | bytes 786440 | tf_op jit(solution)/shard_map/ppermute | solution.py:30
  7.0 18.8 %collective-permute-start.2 = (bf16[2,1,256,256]{3,2,1,0:T(8,128)(2,1)S(1)}, bf16[2,1,256,256]{3,2,1,0:T(8,128)(2,1)S(1)}, u32[]{:S(2)}, u32[]{:S(2)}) collective-permute-start(bf16[2,1,256,256]{3,2,1,0:T(8,128)(2,1)S(1)} %get-tuple-element.36), channel_id=1, source_target_pairs={{0,3},{1,2},{2,1},{3,0},{4,7},{5,6},{6,5},{7,4},{8,11},{9,10},{10,... | collective-permute-start | bytes 786440 | tf_op jit(solution)/shard_map/ppermute | solution.py:30
  8.3 0.7 %copy-start.4 = (u32[32]{0:T(128)S(1)}, u32[32]{0:T(128)}, u32[]{:S(2)}) copy-start(u32[32]{0:T(128)} %constant.37) | copy-start | bytes 388
  8.4 1.8 %copy-start.2 = (bf16[8,1,512]{2,0,1:T(8,128)(2,1)S(1)}, bf16[8,1,512]{2,0,1:T(8,128)(2,1)}, u32[]{:S(2)}) copy-start(bf16[8,1,512]{2,0,1:T(8,128)(2,1)} %param.9) | copy-start | bytes 24580
